TPU v7x, 256 devices: a whole 4x4x8 slice. The times are simulated.
256 devices in a mesh: row: 16 (over z, core), col: 4 (over x), depth: 4 (over y).
Axes of the slice: x: 4, y: 4, z: 8, core: 2. Of those that a mesh axis runs over, the one named last changes fastest.
Arguments:
- residual: float32 [2048, 4096], P(('row', 'depth'), 'col'), may hold values from -4 to 4
- amplitudes: float32 [2048, 65536], P('col', ('row', 'depth')), may hold values from -6 to 6
- integrals: float32 [65536, 4096], P(('row', 'depth'), 'col'), may hold values from -0.0390625 to 0.0390625
- t2_mask: int32 [16, 512], P('col', ('row', 'depth')), may hold values from 0 to 1, as said below
- v_mask: int32 [512, 32], P(('row', 'depth'), 'col'), may hold values from 0 to 1, as said below
Outputs:
- updated: float32 [2048, 4096], P(('row', 'depth'), 'col')
Inputs may be any that keep to these rules, and one draw needn't show every extreme that they name: `t2_mask`: each entry flags one 128 x 128 amplitude tile as kept (1) or zero (0). `v_mask`: each entry flags one 128 x 128 integral tile as kept (1) or zero (0).
All inputs are finite; a program needn't handle non-finite values.
Results may differ from a plain program's by a relative error of at most 0.0001.
Values sent between devices are 32-bit elements; how exact they have to be, the bound alone decides.
A program may use at most 64 MiB of HBM per device.

v0:
```python
import jax
import jax.numpy as jnp
from jax import lax
from jax.sharding import PartitionSpec as P

TILE = 128


def apply_flags(matrix, tile_flags):
    tile_rows, tile_cols = tile_flags.shape
    tiled = (
        matrix.reshape(tile_rows, TILE, tile_cols, TILE)
        * tile_flags.astype(jnp.float32)[:, None, :, None]
    )
    return tiled.reshape(matrix.shape)


def per_device(residual, amplitudes, integrals, t2_mask, v_mask):
    amplitude_kept = apply_flags(amplitudes, t2_mask)
    integral_kept = apply_flags(integrals, v_mask)
    panels = lax.all_gather(amplitude_kept, "col", axis=0, tiled=True)
    summed = lax.psum_scatter(
        jnp.dot(
            panels,
            integral_kept,
            precision=lax.Precision.HIGHEST,
            preferred_element_type=jnp.float32,
        ),
        ("row", "depth"),
        scatter_dimension=0,
        tiled=True,
    )
    return residual + summed


def solution(mesh):
    in_specs = (
        P(("row", "depth"), "col"),
        P("col", ("row", "depth")),
        P(("row", "depth"), "col"),
        P("col", ("row", "depth")),
        P(("row", "depth"), "col"),
    )
    out_specs = P(("row", "depth"), "col")
    return jax.shard_map(
        per_device, mesh=mesh, in_specs=in_specs, out_specs=out_specs, check_vma=False
    )
```

profile of v0, /device:TPU:4, one launch (start us, length us, event | category | flops | bytes accessed | tf_op | source)
XLA Modules:
  0.0 295.0 jit_solution(5104896567255951643)
XLA Ops:
  6.5 0.0 all-gather.2.cloned.1.call-start
  6.5 0.7 convert_element_type.6
  7.2 0.2 mul.22
  7.4 0.0 copy-start.1
  7.4 3.7 %bitcast_multiply_fusion.2 = f32[512,1024]{1,0:T(8,128)} fusion(f32[512,1024]{1,0:T(8,128)} %param.6, f32[64,8,8,128]{3,2,1,0:T(8,128)S(1)} %bitcast.10), kind=kLoop, calls=%fused_computation.3 | loop fusion | flops 524288 | bytes 6291456 | tf_op jit(solution)/shard_map/mul | solution.py:12
  11.1 0.0 all-gather.2.cloned.1.call-update
  11.1 0.0 reduce-scatter.2.cloned.1.call-start
  11.2 0.0 copy-done.1
  11.2 88.4 %all-gather.2.cloned.1.call-done = f32[2048,1024]{1,0:T(8,128)} async-done(((f32[512,1024]{1,0:T(8,128)}), f32[2048,1024]{1,0:T(8,128)}) %all-gather.2.cloned.1.call-update) | async-done | bytes 8388624 | tf_op jit(solution)/shard_map/all_gather | solution.py:21
  99.6 0.0 copy-start.2
  99.6 0.3 mul.25
  99.9 1.8 copy-done.2
  101.8 32.0 %fusion = f32[2048,1024]{1,0:T(8,128)} fusion(f32[2048,1024]{1,0:T(8,128)} %all-gather.2.cloned.1.call-done, f32[1024,1024]{1,0:T(8,128)S(1)} %copy-done.2, f32[128,8,8,128]{3,2,1,0:T(8,128)S(1)} %bitcast.11), kind=kOutput, calls=%fused_computation.1 | convolution fusion | flops 25770852352 | bytes 25165824 | tf_op jit(solution)/shard_map/dot_general | solution.py:23
  133.7 0.0 copy-start
  133.7 0.0 reduce-scatter.2.cloned.1.call-update
  133.8 152.9 %reduce-scatter.2.cloned.1.call-done = f32[32,1024]{1,0:T(8,128)} async-done(((f32[2048,1024]{1,0:T(8,128)}), f32[32,1024]{1,0:T(8,128)}) %reduce-scatter.2.cloned.1.call-update) | async-done | bytes 131088 | tf_op jit(solution)/shard_map/reduce_scatter | solution.py:22
  286.6 0.0 copy-done
  286.6 1.6 add.5
  (1 shorter events, 0.0 us)
Async XLA Ops:
  6.5 93.0 %all-gather.2.cloned.1.call-start = ((), (), s32[]{:S(2)}) async-start(), calls=%async_computation.1 | async-start | bytes 10485760 | tf_op jit(solution)/shard_map/all_gather | solution.py:21
  7.4 3.8 %copy-start.1 = (s32[8,8]{1,0:T(8,128)S(1)}, s32[8,8]{1,0:T(8,128)}, u32[]{:S(2)}) copy-start(s32[8,8]{1,0:T(8,128)} %param.9) | copy-start | bytes 772
  11.1 275.5 %reduce-scatter.2.cloned.1.call-start = ((), (), s32[]{:S(2)}) async-start(), calls=%async_computation.2 | async-start | bytes 8519680 | tf_op jit(solution)/shard_map/reduce_scatter | solution.py:22
  99.6 2.2 copy-start.2
  133.7 152.9 %copy-start = (f32[32,1024]{1,0:T(8,128)S(1)}, f32[32,1024]{1,0:T(8,128)}, u32[]{:S(2)}) copy-start(f32[32,1024]{1,0:T(8,128)} %param.5) | copy-start | bytes 393220
Sparse Core Ops, SparseCore 0:
  11.3 88.2 all-gather.1
  133.9 152.6 reduce-scatter.1
where the time goes:
time: 295 us
  waiting for transfers between devices  241 us (82%)
  matrix products  32 us (11%)
  between operations  13.4 us (5%)
  other arithmetic  5.93 us (2%)
    reduce_scatter x1, waiting for transfers between devices, per_device(): lax.psum_scatter(jnp.dot(panels, integral_kept, precision=lax.Precision.H...  153 us
    all_gather x1, waiting for transfers between devices, per_device(): panels = lax.all_gather(amplitude_kept, 'col', axis=0, tiled=True)  88.4 us
    dot_general x1, matrix products, per_device(): jnp.dot(panels, integral_kept, precision=lax.Precision.HIGHEST, preferred...  32 us
  transfers between devices with their start and end apart: 2, of which 2 were waited for; matrix products, arithmetic and copies ran while one was open for 0% of the time, Pallas kernels for 0%

commit v1 on v0

--- a/solution.py
+++ b/solution.py
@@ -18,7 +18,9 @@
 def per_device(residual, amplitudes, integrals, t2_mask, v_mask):
     amplitude_kept = apply_flags(amplitudes, t2_mask)
     integral_kept = apply_flags(integrals, v_mask)
-    panels = lax.all_gather(amplitude_kept, "col", axis=0, tiled=True)
+    panels = jnp.concatenate(
+        lax.all_to_all(jnp.stack([amplitude_kept] * lax.axis_size("col")), "col", 0, 0), axis=0
+    )
     summed = lax.psum_scatter(
         jnp.dot(
             panels,

time: 295 us -> 309 us (1.047)
  starting transfers between devices: 0.04 us -> 7.98 us
  local copies, waits for them, and re-layouts: 2.39 us -> 6.67 us
    all_to_all x0 -> x1, waiting for transfers between devices: none -> 89.1 us  [per_device(): lax.all_to_all(jnp.stack([amplitude_kept] * lax.axis_size('col')), 'col',...]
    all_gather x1 -> x0, waiting for transfers between devices: 88.4 us -> none  [per_device(): panels = lax.all_gather(amplitude_kept, 'col', axis=0, tiled=True)]
    all_to_all x0 -> x1, starting transfers between devices: none -> 7.97 us  [per_device(): lax.all_to_all(jnp.stack([amplitude_kept] * lax.axis_size('col')), 'col',...]
    another operation x0 -> x1, local copies, waits for them, and re-layouts: none -> 4.28 us  [per_device(): jnp.stack([amplitude_kept] * lax.axis_size('col'))]
where the time goes in v1:
time: 309 us
  waiting for transfers between devices  244 us (79%)
  matrix products  32 us (10%)
  between operations  13.4 us (4%)
  starting transfers between devices  7.98 us (3%)
  local copies, waits for them, and re-layouts  6.67 us (2%)
  other arithmetic  4.57 us (1%)
    reduce_scatter x1, waiting for transfers between devices, per_device(): lax.psum_scatter(jnp.dot(panels, integral_kept, precision=lax.Precision.H...  155 us
    all_to_all x1, waiting for transfers between devices, per_device(): lax.all_to_all(jnp.stack([amplitude_kept] * lax.axis_size('col')), 'col',...  89.1 us
    dot_general x1, matrix products, per_device(): jnp.dot(panels, integral_kept, precision=lax.Precision.HIGHEST, preferred...  32 us
    all_to_all x1, starting transfers between devices, per_device(): lax.all_to_all(jnp.stack([amplitude_kept] * lax.axis_size('col')), 'col',...  7.97 us
  transfers between devices with their start and end apart: 2, of which 2 were waited for; matrix products, arithmetic and copies ran while one was open for 0% of the time, Pallas kernels for 0%

profile of v1, /device:TPU:4, one launch (start us, length us, event | category | flops | bytes accessed | tf_op | source)
XLA Modules:
  0.0 309.1 jit_solution(15325275598445132829)
XLA Ops:
  6.5 0.7 convert_element_type.6
  7.2 0.2 mul.23
  7.4 2.3 bitcast_multiply_fusion.2
  9.7 4.3 %stack.3 = f32[4,512,1024]{2,1,0:T(8,128)} broadcast(f32[512,1024]{1,0:T(8,128)S(1)} %bitcast_multiply_fusion.2), dimensions={1,2} | broadcast | bytes 10485760 | tf_op jit(solution)/shard_map/stack | solution.py:22
  14.0 0.0 copy-start.1
  14.0 8.0 %all-to-all-start = ((f32[4,512,1024]{2,1,0:T(8,128)}), f32[4,512,1024]{2,1,0:T(8,128)}, u32[]{:S(2)}, u32[]{:S(2)}) async-start(f32[4,512,1024]{2,1,0:T(8,128)} %stack.3), calls=%async_computation | async-start | bytes 16777216 | tf_op jit(solution)/shard_map/all_to_all | solution.py:22
  22.0 0.0 reduce-scatter.2.cloned.1.call-start
  22.0 0.0 copy-done.1
  22.0 89.1 %all-to-all-done = f32[4,512,1024]{2,1,0:T(8,128)} async-done(((f32[4,512,1024]{2,1,0:T(8,128)}), f32[4,512,1024]{2,1,0:T(8,128)}, u32[]{:S(2)}, u32[]{:S(2)}) %all-to-all-start) | async-done | bytes 8388640 | tf_op jit(solution)/shard_map/all_to_all | solution.py:22
  111.1 0.0 copy-start.2
  111.1 0.3 mul.26
  111.5 1.8 copy-done.2
  113.3 32.0 %fusion = f32[2048,1024]{1,0:T(8,128)} fusion(f32[2048,1024]{1,0:T(8,128)} %bitcast, f32[1024,1024]{1,0:T(8,128)S(1)} %copy-done.2, f32[128,8,8,128]{3,2,1,0:T(8,128)S(1)} %bitcast.12), kind=kOutput, calls=%fused_computation.1 | convolution fusion | flops 25770852352 | bytes 25165824 | tf_op jit(solution)/shard_map/dot_general | solution.py:25
  145.3 0.0 copy-start
  145.3 0.0 reduce-scatter.2.cloned.1.call-update
  145.3 155.3 %reduce-scatter.2.cloned.1.call-done = f32[32,1024]{1,0:T(8,128)} async-done(((f32[2048,1024]{1,0:T(8,128)}), f32[32,1024]{1,0:T(8,128)}) %reduce-scatter.2.cloned.1.call-update) | async-done | bytes 131088 | tf_op jit(solution)/shard_map/reduce_scatter | solution.py:24
  300.6 0.0 copy-done
  300.6 1.6 add.5
  (1 shorter events, 0.0 us)
Async XLA Ops:
  14.0 8.0 %copy-start.1 = (s32[8,8]{1,0:T(8,128)S(1)}, s32[8,8]{1,0:T(8,128)}, u32[]{:S(2)}) copy-start(s32[8,8]{1,0:T(8,128)} %param.9) | copy-start | bytes 772
  14.0 97.1 %all-to-all-start = ((f32[4,512,1024]{2,1,0:T(8,128)}), f32[4,512,1024]{2,1,0:T(8,128)}, u32[]{:S(2)}, u32[]{:S(2)}) async-start(f32[4,512,1024]{2,1,0:T(8,128)} %stack.3), calls=%async_computation | async-start | bytes 16777216 | tf_op jit(solution)/shard_map/all_to_all | solution.py:22
  22.0 278.6 %reduce-scatter.2.cloned.1.call-start = ((), (), s32[]{:S(2)}) async-start(), calls=%async_computation.2 | async-start | bytes 8519680 | tf_op jit(solution)/shard_map/reduce_scatter | solution.py:24
  111.1 2.2 copy-start.2
  145.3 155.3 %copy-start = (f32[32,1024]{1,0:T(8,128)S(1)}, f32[32,1024]{1,0:T(8,128)}, u32[]{:S(2)}) copy-start(f32[32,1024]{1,0:T(8,128)} %param.5) | copy-start | bytes 393220
Sparse Core Ops, SparseCore 0:
  145.4 155.1 reduce-scatter.1
